TPU v7x, 32 devices: a whole 2x2x4 slice. The times are simulated.
32 devices in a mesh: dp: 8 (over z, y), expert: 4 (over x, core).
Axes of the slice: x: 2, y: 2, z: 4, core: 2. Of those that a mesh axis runs over, the one named last changes fastest.
Arguments:
- tokens: bfloat16 [4096, 1024], P(('dp', 'expert')), may hold values from -6 to 6
- cotangent: bfloat16 [4096, 1024], P(('dp', 'expert')), may hold values from -6 to 6
- expert_ids: int32 [4096, 2], P(('dp', 'expert')), may hold values from 0 to 3, all different within a row; in each aligned block of 128 rows (0 to 127, 128 to 255, ...) at most 128 rows name the same one
- gate_weights: float32 [4096, 2], P(('dp', 'expert')), may hold values from 0.05 to 1
- w_gate: bfloat16 [4, 384, 1024], P('expert'), may hold values from -0.1875 to 0.1875
- w_up: bfloat16 [4, 384, 1024], P('expert'), may hold values from -0.1875 to 0.1875
- w_down: bfloat16 [4, 384, 1024], P('expert'), may hold values from -0.3125 to 0.3125
Outputs:
- layer_out: bfloat16 [4096, 1024], P(('dp', 'expert'))
- grad_tokens: bfloat16 [4096, 1024], P(('dp', 'expert'))
- grad_up: float32 [4, 384, 1024], P('expert', 'dp')
- grad_down: float32 [4, 384, 1024], P('expert', 'dp')
Inputs may be any that keep to these rules, and one draw needn't show every extreme that they name: `expert_ids`: each row names 2 different experts. Among the 128 rows of one device no expert is named more than 128 times, and in every draw some expert is named exactly 128 times by the rows of some device.
All inputs are finite; a program needn't handle non-finite values.
Results may differ from a plain program's by a relative error of at most 0.0065.
Values may be sent and summed in bfloat16 or wider, within the bound.
A program may use at most 64 MiB of HBM per device.

v0:
```python
import jax
import jax.numpy as jnp
from jax import lax
from jax.sharding import PartitionSpec as P


def batched(left_op, right_op, left_dim, right_dim):
    return lax.dot_general(
        left_op,
        right_op,
        (((left_dim,), (right_dim,)), ((0,), (0,))),
        preferred_element_type=jnp.float32,
    )


def forward(received, w_gate, w_up, w_down):
    gate_pre = batched(received, w_gate, 2, 2)
    up_pre = batched(received, w_up, 2, 2)
    gate_sig = jax.nn.sigmoid(gate_pre)
    hidden = (gate_pre * gate_sig * up_pre).astype(jnp.bfloat16)
    expert_out = batched(hidden, w_down, 2, 1).astype(jnp.bfloat16)
    return ((gate_pre, up_pre, gate_sig, hidden), expert_out)


def backward(received, grad_out, saved_acts, w_gate, w_up, w_down):
    gate_pre, up_pre, gate_sig, hidden = saved_acts
    grad_lower = lax.psum_scatter(
        batched(hidden, grad_out, 1, 1), "dp", scatter_dimension=1, tiled=True
    )
    grad_hidden = batched(grad_out, w_down, 2, 2)
    grad_up_pre = (grad_hidden * gate_pre * gate_sig).astype(jnp.bfloat16)
    grad_gate_pre = (grad_hidden * up_pre * gate_sig * (1.0 + gate_pre * (1.0 - gate_sig))).astype(
        jnp.bfloat16
    )
    grad_input = (batched(grad_gate_pre, w_gate, 2, 1) + batched(grad_up_pre, w_up, 2, 1)).astype(
        jnp.bfloat16
    )
    grad_upper = batched(grad_up_pre, received, 1, 1)
    grad_upper = lax.psum_scatter(grad_upper, "dp", scatter_dimension=1, tiled=True)
    return (grad_input, (grad_upper, grad_lower))


def shards(tokens, cotangent, expert_ids, gate_weights, w_gate, w_up, w_down):
    tok_rows, model_width = tokens.shape
    top_count = expert_ids.shape[1]
    local_experts = w_gate.shape[0]
    groups = lax.axis_size("expert")
    experts = local_experts * groups
    capacity = 2 * tok_rows * top_count // experts
    pair_count = tok_rows * top_count
    slot_count = experts * capacity
    flat_ids = expert_ids.reshape(-1)
    flat_gates = gate_weights.reshape(-1)
    onehot = (flat_ids[:, None] == jnp.arange(experts, dtype=jnp.int32)[None, :]).astype(jnp.int32)
    before = jnp.cumsum(onehot, axis=0) - onehot
    slot_rank = jnp.sum(before * onehot, axis=1)
    position = flat_ids * capacity + slot_rank
    matches = position[None, :] == jnp.arange(slot_count, dtype=jnp.int32)[:, None]
    source = (
        jnp.sum(jnp.where(matches, jnp.arange(pair_count, dtype=jnp.int32)[None, :] + 1, 0), axis=1)
        - 1
    )
    filled = source >= 0
    clipped = jnp.maximum(source, 0)
    token_rows = clipped // top_count
    slot_gates = jnp.where(filled, flat_gates[clipped], 0.0)
    sent_tokens = jnp.where(filled[:, None], tokens[token_rows], jnp.zeros((), jnp.bfloat16))
    sent_tokens = sent_tokens.reshape(experts, capacity, model_width)
    sent_grads = (slot_gates[:, None] * cotangent[token_rows].astype(jnp.float32)).astype(
        jnp.bfloat16
    )
    sent_grads = sent_grads.reshape(experts, capacity, model_width)
    received = lax.all_to_all(sent_tokens, "expert", split_axis=0, concat_axis=1, tiled=True)
    saved_acts, expert_out = forward(received, w_gate, w_up, w_down)
    back_out = lax.all_to_all(expert_out, "expert", split_axis=1, concat_axis=0, tiled=True)
    grad_out = lax.all_to_all(sent_grads, "expert", split_axis=0, concat_axis=1, tiled=True)
    grad_input, grads = backward(received, grad_out, saved_acts, w_gate, w_up, w_down)
    back_grad = lax.all_to_all(grad_input, "expert", split_axis=1, concat_axis=0, tiled=True)
    out_rows = (
        back_out.reshape(slot_count, model_width)[position].astype(jnp.float32)
        * flat_gates[:, None]
    )
    layer_out = jnp.sum(out_rows.reshape(tok_rows, top_count, model_width), axis=1).astype(
        jnp.bfloat16
    )
    grad_rows = back_grad.reshape(slot_count, model_width)[position].astype(jnp.float32)
    grad_tokens = jnp.sum(grad_rows.reshape(tok_rows, top_count, model_width), axis=1).astype(
        jnp.bfloat16
    )
    grad_scale = (tok_rows * lax.axis_size("dp") * groups * top_count / experts) ** (-0.5)
    return (layer_out, grad_tokens, grads[0] * grad_scale, grads[1] * grad_scale)


def solution(mesh):
    in_specs = (
        P(("dp", "expert"), None),
        P(("dp", "expert"), None),
        P(("dp", "expert"), None),
        P(("dp", "expert"), None),
        P("expert", None, None),
        P("expert", None, None),
        P("expert", None, None),
    )
    out_specs = (
        P(("dp", "expert"), None),
        P(("dp", "expert"), None),
        P("expert", "dp", None),
        P("expert", "dp", None),
    )
    return jax.shard_map(shards, mesh=mesh, in_specs=in_specs, out_specs=out_specs, check_vma=False)
```

profile of v0, /device:TPU:0, one launch (start us, length us, event | category | flops | bytes accessed | tf_op | source)
XLA Modules:
  0.0 203.4 jit_solution(15513453985991420824)
XLA Ops:
  7.2 0.0 copy-start
  7.2 0.9 copy.39
  8.1 0.1 eq.39
  8.2 0.1 reshape.250
  8.4 1.2 reduce-window.6
  9.6 0.1 slice.18
  9.7 0.1 copy.41
  9.8 0.1 copy.42
  9.9 0.1 add_bitcast_fusion
  10.0 0.2 select_reduce_fusion
  10.2 0.8 copy.45
  11.0 0.1 reshape.257
  11.1 3.5 %gather_fusion.2 = f32[512]{0:T(512)S(1)} fusion(f32[256]{0:T(256)S(1)} %reshape.257, s32[1024]{0:T(1024)S(1)} %pad_clamp_fusion), kind=kCustom, calls=%fused_computation.2 | custom fusion | bytes 6144 | tf_op jit(solution)/shard_map/gather | solution.py:66
  14.7 2.1 %gather_fusion = bf16[512,1024]{1,0:T(8,128)(2,1)S(1)} fusion(bf16[128,1024]{1,0:T(8,128)(2,1)S(1)} %copy-done.1, s32[1024]{0:T(1024)S(1)} %pad_clamp_fusion.2), kind=kCustom, calls=%fused_computation | custom fusion | bytes 2099200 | tf_op jit(solution)/shard_map/gather | solution.py:67
  16.8 1.2 broadcast_select_fusion
  18.0 4.2 %all-to-all-start = ((bf16[4,128,1024]{2,1,0:T(8,128)(2,1)}), bf16[4,128,1024]{2,1,0:T(8,128)(2,1)S(1)}, u32[]{:S(2)}, u32[]{:S(2)}) async-start(bf16[4,128,1024]{2,1,0:T(8,128)(2,1)} %broadcast_select_fusion), calls=%async_computation | async-start | bytes 2097152 | tf_op jit(solution)/shard_map/all_to_all | solution.py:73
  22.2 2.0 %gather_fusion.3 = bf16[512,1024]{1,0:T(8,128)(2,1)S(1)} fusion(bf16[128,1024]{1,0:T(8,128)(2,1)S(1)} %copy-done.2, s32[1024]{0:T(1024)S(1)} %pad_clamp_fusion.2), kind=kCustom, calls=%fused_computation.3 | custom fusion | bytes 2099200 | tf_op jit(solution)/shard_map/gather | solution.py:69
  24.3 1.2 fusion
  25.5 11.1 %all-to-all-done = bf16[4,128,1024]{2,1,0:T(8,128)(2,1)S(1)} async-done(((bf16[4,128,1024]{2,1,0:T(8,128)(2,1)}), bf16[4,128,1024]{2,1,0:T(8,128)(2,1)S(1)}, u32[]{:S(2)}, u32[]{:S(2)}) %all-to-all-start) | async-done | bytes 1048608 | tf_op jit(solution)/shard_map/all_to_all | solution.py:73
  36.6 3.5 %all-to-all-start.2 = ((bf16[4,128,1024]{2,1,0:T(8,128)(2,1)}), bf16[4,128,1024]{2,1,0:T(8,128)(2,1)S(1)}, u32[]{:S(2)}, u32[]{:S(2)}) async-start(bf16[4,128,1024]{2,1,0:T(8,128)(2,1)} %fusion), calls=%async_computation.2 | async-start | bytes 2097152 | tf_op jit(solution)/shard_map/all_to_all | solution.py:76
  40.1 0.0 reduce-scatter.5.cloned.1.call-start
  40.2 0.0 copy-start.3
  40.2 2.9 %fusion.11 = f32[512,384]{1,0:T(8,128)} fusion(bf16[512,1024]{1,0:T(8,128)(2,1)S(1)} %bitcast.83, bf16[1,384,1024]{2,1,0:T(8,128)(2,1)} %param.11), kind=kOutput, calls=%fused_computation.25 | convolution fusion | flops 402653184 | bytes 2621440 | tf_op jit(solution)/shard_map/dot_general | solution.py:8
  43.1 1.6 fusion.7
  44.7 9.8 %all-to-all-done.2 = bf16[4,128,1024]{2,1,0:T(8,128)(2,1)S(1)} async-done(((bf16[4,128,1024]{2,1,0:T(8,128)(2,1)}), bf16[4,128,1024]{2,1,0:T(8,128)(2,1)S(1)}, u32[]{:S(2)}, u32[]{:S(2)}) %all-to-all-start.2) | async-done | bytes 1048608 | tf_op jit(solution)/shard_map/all_to_all | solution.py:76
  54.5 3.0 %multiply_convert_fusion = (bf16[512,384]{1,0:T(8,128)(2,1)S(1)}, bf16[512,384]{1,0:T(8,128)(2,1)S(1)}, f32[512,384]{1,0:T(8,128)}) fusion(f32[512,384]{1,0:T(8,128)} %fusion.11, f32[512,384]{1,0:T(8,128)} %fusion.7, bf16[512,1024]{1,0:T(8,128)(2,1)S(1)} %bitcast.92, bf16[1,384,1024]{2,1,0:T(8,128)(2,1)S(1)} %copy-done), kind=kOutput, calls=%fused_computation.27 | convolution fusion | flops 404422656 | bytes 4980736 | tf_op jit(solution)/shard_map/dot_general | solution.py:8
  57.5 0.8 copy-done.5
  58.3 1.8 convolution_bitcast_fusion
  60.1 0.0 reduce-scatter.5.cloned.1.call-update
  60.1 0.2 reduce-scatter.3.cloned.1.call-start
  60.3 0.0 copy-start.7
  60.4 1.7 convolution_bitcast_fusion.1
  62.1 0.0 reduce-scatter.3.cloned.1.call-update
  62.1 0.0 copy-start.4
  62.1 2.6 %fusion.9 = f32[512,1024]{1,0:T(8,128)S(1)} fusion(bf16[1,384,1024]{2,1,0:T(8,128)(2,1)S(1)} %copy-done.7, f32[512,384]{1,0:T(8,128)} %fusion.11, f32[512,384]{1,0:T(8,128)} %get-tuple-element.10, f32[512,384]{1,0:T(8,128)} %fusion.7), kind=kOutput, calls=%fused_computation.23 | convolution fusion | flops 404619264 | bytes 5242880 | tf_op jit(solution)/shard_map/dot_general | solution.py:8
  64.7 0.7 fusion.2
  65.4 1.6 copy.58
  67.1 0.5 broadcast.255
  67.6 7.8 %reduce.2 = bf16[512,1024]{1,0:T(8,128)(2,1)} reduce(bf16[512,1,1024]{2,1,0:T(2,128)(2,1)S(1)} %bitcast.88, bf16[]{:T(256)} %broadcast.255), dimensions={1}, to_apply=%bitcast.79.reduce_sub_computation | reduce | bytes 2097154
  75.4 3.8 %reshape.318 = bf16[4,2,65536]{2,1,0:T(2,128)(2,1)} reshape(bf16[512,1024]{1,0:T(8,128)(2,1)} %reduce.2) | data formatting | bytes 2097152
  79.2 4.5 %all-to-all-start.3 = ((bf16[4,2,65536]{2,1,0:T(2,128)(2,1)}), bf16[4,2,65536]{2,1,0:T(2,128)(2,1)}, u32[]{:S(2)}, u32[]{:S(2)}) async-start(bf16[4,2,65536]{2,1,0:T(2,128)(2,1)} %reshape.318), calls=%async_computation.3 | async-start | bytes 2097152 | tf_op jit(solution)/shard_map/all_to_all | solution.py:78
  83.7 0.7 fusion.1
  84.4 1.6 copy.59
  86.0 7.8 %reduce.1 = bf16[512,1024]{1,0:T(8,128)(2,1)} reduce(bf16[512,1,1024]{2,1,0:T(2,128)(2,1)S(1)} %bitcast.89, bf16[]{:T(256)} %broadcast.255), dimensions={1}, to_apply=%bitcast.80.reduce_sub_computation | reduce | bytes 2097154
  93.8 3.7 %reshape.316 = bf16[4,2,65536]{2,1,0:T(2,128)(2,1)} reshape(bf16[512,1024]{1,0:T(8,128)(2,1)} %reduce.1) | data formatting | bytes 2097152
  97.6 0.3 all-to-all-done.3
  97.9 3.8 %all-to-all-start.1 = ((bf16[4,2,65536]{2,1,0:T(2,128)(2,1)}), bf16[4,2,65536]{2,1,0:T(2,128)(2,1)S(1)}, u32[]{:S(2)}, u32[]{:S(2)}) async-start(bf16[4,2,65536]{2,1,0:T(2,128)(2,1)} %reshape.316), calls=%async_computation.1 | async-start | bytes 2097152 | tf_op jit(solution)/shard_map/all_to_all | solution.py:75
  101.7 0.1 copy.44
  101.9 0.1 mul.90
  102.0 4.0 %reshape.319 = bf16[512,1,1024]{2,1,0:T(2,128)(2,1)} reshape(bf16[4,2,65536]{2,1,0:T(2,128)(2,1)} %all-to-all-done.3) | data formatting | bytes 2097152
  106.0 2.0 copy.56
  108.0 1.2 gather_fusion.4
  109.1 0.2 gather.28
  109.4 6.5 %all-to-all-done.1 = bf16[4,2,65536]{2,1,0:T(2,128)(2,1)S(1)} async-done(((bf16[4,2,65536]{2,1,0:T(2,128)(2,1)}), bf16[4,2,65536]{2,1,0:T(2,128)(2,1)S(1)}, u32[]{:S(2)}, u32[]{:S(2)}) %all-to-all-start.1) | async-done | bytes 1048608 | tf_op jit(solution)/shard_map/all_to_all | solution.py:75
  115.9 2.3 %reshape.317 = bf16[512,1,1024]{2,1,0:T(2,128)(2,1)} reshape(bf16[4,2,65536]{2,1,0:T(2,128)(2,1)S(1)} %all-to-all-done.1) | data formatting | bytes 2097152
  118.2 2.0 copy.57
  120.2 1.2 gather_fusion.1
  121.3 0.7 reshape.260
  122.0 2.1 %reduce_sum.45 = bf16[128,1024]{1,0:T(8,128)(2,1)} reduce(bf16[128,2,1024]{2,1,0:T(2,128)(2,1)S(1)} %gather.28, bf16[]{:T(256)} %constant.37.clone.1), dimensions={1}, to_apply=%region_5.6 | reduce | flops 131072 | bytes 786434 | tf_op jit(solution)/shard_map/reduce_sum | solution.py:87
  124.1 2.1 %multiply_reduce_fusion = bf16[128,1024]{1,0:T(8,128)(2,1)} fusion(f32[128,2,1024]{2,1,0:T(2,128)S(1)} %reshape.260, f32[128,2]{1,0:T(8,128)S(1)} %copy.45), kind=kLoop, calls=%fused_computation.15 | loop fusion | flops 393216 | bytes 1311744 | tf_op jit(solution)/shard_map/reduce_sum | solution.py:83
  126.2 0.9 reduce-scatter.5.cloned.1.call-done
  127.1 1.6 broadcast_multiply_fusion
  128.7 66.2 %reduce-scatter.3.cloned.1.call-done = f32[1,48,1024]{2,1,0:T(8,128)} async-done(((f32[1,384,1024]{2,1,0:T(8,128)}), f32[1,48,1024]{2,1,0:T(8,128)}) %reduce-scatter.3.cloned.1.call-update) | async-done | bytes 196624 | tf_op jit(solution)/shard_map/reduce_scatter | solution.py:39
  194.9 1.6 broadcast_multiply_fusion.1
  (27 shorter events, 0.2 us)
Async XLA Ops:
  7.2 47.4 %copy-start = (bf16[1,384,1024]{2,1,0:T(8,128)(2,1)S(1)}, bf16[1,384,1024]{2,1,0:T(8,128)(2,1)}, u32[]{:S(2)}) copy-start(bf16[1,384,1024]{2,1,0:T(8,128)(2,1)} %param.13) | copy-start | bytes 2359300
  7.2 7.5 %copy-start.1 = (bf16[128,1024]{1,0:T(8,128)(2,1)S(1)}, bf16[128,1024]{1,0:T(8,128)(2,1)}, u32[]{:S(2)}) copy-start(bf16[128,1024]{1,0:T(8,128)(2,1)} %param.7) | copy-start | bytes 786436
  16.8 5.4 %copy-start.2 = (bf16[128,1024]{1,0:T(8,128)(2,1)S(1)}, bf16[128,1024]{1,0:T(8,128)(2,1)}, u32[]{:S(2)}) copy-start(bf16[128,1024]{1,0:T(8,128)(2,1)} %param.8) | copy-start | bytes 786436
  18.0 18.7 %all-to-all-start = ((bf16[4,128,1024]{2,1,0:T(8,128)(2,1)}), bf16[4,128,1024]{2,1,0:T(8,128)(2,1)S(1)}, u32[]{:S(2)}, u32[]{:S(2)}) async-start(bf16[4,128,1024]{2,1,0:T(8,128)(2,1)} %broadcast_select_fusion), calls=%async_computation | async-start | bytes 2097152 | tf_op jit(solution)/shard_map/all_to_all | solution.py:73
  36.6 17.9 %all-to-all-start.2 = ((bf16[4,128,1024]{2,1,0:T(8,128)(2,1)}), bf16[4,128,1024]{2,1,0:T(8,128)(2,1)S(1)}, u32[]{:S(2)}, u32[]{:S(2)}) async-start(bf16[4,128,1024]{2,1,0:T(8,128)(2,1)} %fusion), calls=%async_computation.2 | async-start | bytes 2097152 | tf_op jit(solution)/shard_map/all_to_all | solution.py:76
  40.1 86.9 %reduce-scatter.5.cloned.1.call-start = ((), (), s32[]{:S(2)}) async-start(), calls=%async_computation.7 | async-start | bytes 1769472 | tf_op jit(solution)/shard_map/reduce_scatter | solution.py:27
  40.2 2.9 %copy-start.3 = (bf16[1,384,1024]{2,1,0:T(8,128)(2,1)S(1)}, bf16[1,384,1024]{2,1,0:T(8,128)(2,1)}, u32[]{:S(2)}) copy-start(bf16[1,384,1024]{2,1,0:T(8,128)(2,1)} %param.12) | copy-start | bytes 2359300
  57.5 0.8 copy-start.5
  60.1 134.8 %reduce-scatter.3.cloned.1.call-start = ((), (), s32[]{:S(2)}) async-start(), calls=%async_computation.6 | async-start | bytes 1769472 | tf_op jit(solution)/shard_map/reduce_scatter | solution.py:39
  60.3 1.8 copy-start.7
  62.1 2.6 %copy-start.4 = (bf16[1,384,1024]{2,1,0:T(8,128)(2,1)S(1)}, bf16[1,384,1024]{2,1,0:T(8,128)(2,1)}, u32[]{:S(2)}) copy-start(bf16[1,384,1024]{2,1,0:T(8,128)(2,1)} %param.12) | copy-start | bytes 2359300
  75.4 8.3 %copy-start.6 = (bf16[512,384]{1,0:T(8,128)(2,1)S(1)}, bf16[512,384]{1,0:T(8,128)(2,1)}, u32[]{:S(2)}) copy-start(bf16[512,384]{1,0:T(8,128)(2,1)} %copy-done.5) | copy-start | bytes 1179652
  79.2 18.8 %all-to-all-start.3 = ((bf16[4,2,65536]{2,1,0:T(2,128)(2,1)}), bf16[4,2,65536]{2,1,0:T(2,128)(2,1)}, u32[]{:S(2)}, u32[]{:S(2)}) async-start(bf16[4,2,65536]{2,1,0:T(2,128)(2,1)} %reshape.318), calls=%async_computation.3 | async-start | bytes 2097152 | tf_op jit(solution)/shard_map/all_to_all | solution.py:78
  93.8 7.9 %copy-start.8 = (s32[128,2]{0,1:T(2,128)S(1)}, s32[128,2]{0,1:T(2,128)}, u32[]{:S(2)}) copy-start(s32[128,2]{0,1:T(2,128)} %param.9) | copy-start | bytes 3076
  97.9 17.9 %all-to-all-start.1 = ((bf16[4,2,65536]{2,1,0:T(2,128)(2,1)}), bf16[4,2,65536]{2,1,0:T(2,128)(2,1)S(1)}, u32[]{:S(2)}, u32[]{:S(2)}) async-start(bf16[4,2,65536]{2,1,0:T(2,128)(2,1)} %reshape.316), calls=%async_computation.1 | async-start | bytes 2097152 | tf_op jit(solution)/shard_map/all_to_all | solution.py:75
Sparse Core Ops, SparseCore 0:
  60.2 66.8 reduce-scatter.4
  130.5 64.3 reduce-scatter.2
where the time goes:
time: 204 us; the launch traced here: 203 us
  waiting for transfers between devices  95 us (47%)
  local copies, waits for them, and re-layouts  35.7 us (18%)
  other arithmetic  27 us (13%)
  starting transfers between devices  16.3 us (8%)
  matrix products  15 us (7%)
  between operations  14.3 us (7%)
    reduce_scatter x1, waiting for transfers between devices, backward(): lax.psum_scatter(grad_upper, 'dp', scatter_dimension=1, tiled=True)  66.2 us
    unnamed x27, local copies, waits for them, and re-layouts  20.8 us
    unnamed x3, other arithmetic  15.7 us
    dot_general x8, matrix products, batched(): lax.dot_general(left_op, right_op, (((left_dim,), (right_dim,)), ((0,), (...  15 us
    all_to_all x1, waiting for transfers between devices, shards(): lax.all_to_all(sent_tokens, 'expert', split_axis=0, concat_axis=1, tiled=...  11.1 us
    all_to_all x1, waiting for transfers between devices, shards(): lax.all_to_all(sent_grads, 'expert', split_axis=0, concat_axis=1, tiled=T...  9.83 us
    all_to_all x1, waiting for transfers between devices, shards(): lax.all_to_all(expert_out, 'expert', split_axis=1, concat_axis=0, tiled=T...  6.51 us
    all_to_all x1, starting transfers between devices, shards(): lax.all_to_all(grad_input, 'expert', split_axis=1, concat_axis=0, tiled=T...  4.48 us
  transfers between devices with their start and end apart: 6, of which 6 were waited for; matrix products, arithmetic and copies ran while one was open for 29% of the time, Pallas kernels for 0%

commit v1 on v0

--- a/solution.py
+++ b/solution.py
@@ -70,7 +70,15 @@
         jnp.bfloat16
     )
     sent_grads = sent_grads.reshape(experts, capacity, model_width)
-    received = lax.all_to_all(sent_tokens, "expert", split_axis=0, concat_axis=1, tiled=True)
+    ways, here = (lax.axis_size("expert"), lax.axis_index("expert"))
+    width = sent_tokens.shape[0] // ways
+    turned = jnp.roll(sent_tokens, -here * width, axis=0)
+    got = [lax.slice_in_dim(turned, 0, width, axis=0)]
+    for far in range(1, ways):
+        sent = lax.slice_in_dim(turned, far * width, (far + 1) * width, axis=0)
+        got.append(lax.ppermute(sent, "expert", [(d, (d + far) % ways) for d in range(ways)]))
+    line = jnp.concatenate(got[::-1], axis=1)
+    received = jnp.roll(line, (here + 1) * got[0].shape[1], axis=1)
     saved_acts, expert_out = forward(received, w_gate, w_up, w_down)
     back_out = lax.all_to_all(expert_out, "expert", split_axis=1, concat_axis=0, tiled=True)
     grad_out = lax.all_to_all(sent_grads, "expert", split_axis=0, concat_axis=1, tiled=True)

time: 204 us -> 196 us (0.961)
  waiting for transfers between devices: 95 us -> 81.7 us
  local copies, waits for them, and re-layouts: 35.7 us -> 40.8 us
    reduce_scatter x1, waiting for transfers between devices: 66.2 us -> 0.01 us  [backward(): lax.psum_scatter(grad_upper, 'dp', scatter_dimension=1, tiled=True)]
    reduce_scatter x1, waiting for transfers between devices: 0.94 us -> 66 us  [backward(): lax.psum_scatter(batched(hidden, grad_out, 1, 1), 'dp', scatter_dimension...]
    all_to_all x1 -> x0, waiting for transfers between devices: 11.1 us -> none  [shards(): lax.all_to_all(sent_tokens, 'expert', split_axis=0, concat_axis=1, tiled=...]
    all_to_all x1, waiting for transfers between devices: 9.83 us -> 3.84 us  [shards(): lax.all_to_all(sent_grads, 'expert', split_axis=0, concat_axis=1, tiled=T...]
    ppermute x0 -> x3, waiting for transfers between devices: none -> 4.98 us  [shards(): lax.ppermute(sent, 'expert', [(d, (d + far) % ways) for d in range(ways)])]
    all_to_all x1 -> x0, starting transfers between devices: 4.24 us -> none  [shards(): lax.all_to_all(sent_tokens, 'expert', split_axis=0, concat_axis=1, tiled=...]
    unnamed x27 -> x38, local copies, waits for them, and re-layouts: 20.8 us -> 24 us
    ppermute x0 -> x3, starting transfers between devices: none -> 3.2 us  [shards(): lax.ppermute(sent, 'expert', [(d, (d + far) % ways) for d in range(ways)])]
  transfers between devices with their start and end apart: 6 -> 8, of which waited for: 6 -> 6; matrix products, arithmetic and copies ran while one was open for 29% -> 33% of each run, Pallas kernels for 0% -> 0%
where the time goes in v1:
time: 196 us; the launch traced here: 195 us
  waiting for transfers between devices  81.7 us (42%)
  local copies, waits for them, and re-layouts  40.8 us (21%)
  other arithmetic  26.4 us (13%)
  starting transfers between devices  15.9 us (8%)
  matrix products  15.5 us (8%)
  between operations  14.5 us (7%)
    reduce_scatter x1, waiting for transfers between devices, backward(): lax.psum_scatter(batched(hidden, grad_out, 1, 1), 'dp', scatter_dimension...  66 us
    unnamed x38, local copies, waits for them, and re-layouts  24 us
    unnamed x3, other arithmetic  15.7 us
    dot_general x8, matrix products, batched(): lax.dot_general(left_op, right_op, (((left_dim,), (right_dim,)), ((0,), (...  15.5 us
    all_to_all x1, waiting for transfers between devices, shards(): lax.all_to_all(expert_out, 'expert', split_axis=1, concat_axis=0, tiled=T...  6.53 us
    ppermute x3, waiting for transfers between devices, shards(): lax.ppermute(sent, 'expert', [(d, (d + far) % ways) for d in range(ways)])  4.98 us
    all_to_all x1, starting transfers between devices, shards(): lax.all_to_all(grad_input, 'expert', split_axis=1, concat_axis=0, tiled=T...  4.47 us
    all_to_all x1, starting transfers between devices, shards(): lax.all_to_all(sent_grads, 'expert', split_axis=0, concat_axis=1, tiled=T...  4.23 us
  transfers between devices with their start and end apart: 8, of which 6 were waited for; matrix products, arithmetic and copies ran while one was open for 33% of the time, Pallas kernels for 0%

profile of v1, /device:TPU:0, one launch (start us, length us, event | category | flops | bytes accessed | tf_op | source)
XLA Modules:
  0.0 194.8 jit_solution(16646785315246334690)
XLA Ops:
  7.2 0.9 copy.39
  8.1 0.1 eq.44
  8.2 0.1 reshape.244
  8.4 1.2 reduce-window.6
  9.6 0.1 slice.34
  9.7 0.1 copy.41
  9.8 0.1 copy.42
  10.0 0.2 select_reduce_fusion
  10.2 0.8 copy.45
  11.0 0.1 reshape.251
  11.2 3.5 %gather_fusion.2 = f32[512]{0:T(512)S(1)} fusion(f32[256]{0:T(256)S(1)} %reshape.251, s32[1024]{0:T(1024)S(1)} %pad_clamp_fusion), kind=kCustom, calls=%fused_computation.2 | custom fusion | bytes 6144 | tf_op jit(solution)/shard_map/gather | solution.py:66
  14.7 2.1 %gather_fusion = bf16[512,1024]{1,0:T(8,128)(2,1)S(1)} fusion(bf16[128,1024]{1,0:T(8,128)(2,1)S(1)} %copy-done.1, s32[1024]{0:T(1024)S(1)} %pad_clamp_fusion.2), kind=kCustom, calls=%fused_computation | custom fusion | bytes 2099200 | tf_op jit(solution)/shard_map/gather | solution.py:67
  16.8 0.1 broadcast_select_fusion
  17.0 0.4 fusion.3
  17.4 1.0 copy-done.3
  18.4 0.9 fusion.29
  19.2 2.4 %collective-permute-start = (bf16[1,128,1024]{2,1,0:T(8,128)(2,1)S(1)}, bf16[1,128,1024]{2,1,0:T(8,128)(2,1)S(1)}, u32[]{:S(2)}, u32[]{:S(2)}) collective-permute-start(bf16[1,128,1024]{2,1,0:T(8,128)(2,1)S(1)} %get-tuple-element.8), channel_id=1, source_target_pairs={{0,3},{1,0},{2,1},{3,2},{4,7},{5,4},{6,5},{7,6},{8,11},{9,8},{10,9... | collective-permute-start | bytes 786440 | tf_op jit(solution)/shard_map/ppermute | solution.py:79
  21.6 0.6 collective-permute-start.1
  22.2 0.2 collective-permute-start.2
  22.4 2.0 %gather_fusion.3 = bf16[512,1024]{1,0:T(8,128)(2,1)S(1)} fusion(bf16[128,1024]{1,0:T(8,128)(2,1)S(1)} %copy-done.2, s32[1024]{0:T(1024)S(1)} %pad_clamp_fusion.2), kind=kCustom, calls=%fused_computation.3 | custom fusion | bytes 2099200 | tf_op jit(solution)/shard_map/gather | solution.py:69
  24.5 1.3 fusion
  25.7 4.2 %all-to-all-start.1 = ((bf16[4,128,1024]{2,1,0:T(8,128)(2,1)}), bf16[4,128,1024]{2,1,0:T(8,128)(2,1)}, u32[]{:S(2)}, u32[]{:S(2)}) async-start(bf16[4,128,1024]{2,1,0:T(8,128)(2,1)} %fusion), calls=%async_computation.1 | async-start | bytes 2097152 | tf_op jit(solution)/shard_map/all_to_all | solution.py:84
  30.1 4.8 %collective-permute-done.1 = bf16[1,128,1024]{2,1,0:T(8,128)(2,1)S(1)} collective-permute-done((bf16[1,128,1024]{2,1,0:T(8,128)(2,1)}, bf16[1,128,1024]{2,1,0:T(8,128)(2,1)S(1)}, u32[]{:S(2)}, u32[]{:S(2)}) %collective-permute-start.1) | collective-permute-done | bytes 262176 | tf_op jit(solution)/shard_map/ppermute | solution.py:79
  34.9 0.1 collective-permute-done.2
  35.1 1.0 constant_dynamic-update-slice_fusion.3
  36.1 1.0 slice_dynamic-update-slice_fusion
  37.1 1.0 constant_dynamic-update-slice_fusion
  38.1 1.0 slice_dynamic-update-slice_fusion.1
  39.1 1.6 fusion.5
  40.8 1.7 fusion.7
  42.4 3.8 %all-to-all-done.1 = bf16[4,128,1024]{2,1,0:T(8,128)(2,1)} async-done(((bf16[4,128,1024]{2,1,0:T(8,128)(2,1)}), bf16[4,128,1024]{2,1,0:T(8,128)(2,1)}, u32[]{:S(2)}, u32[]{:S(2)}) %all-to-all-start.1) | async-done | bytes 1048608 | tf_op jit(solution)/shard_map/all_to_all | solution.py:84
  46.3 3.5 %multiply_convert_fusion = (bf16[512,384]{1,0:T(8,128)(2,1)S(1)}, bf16[512,384]{1,0:T(8,128)(2,1)}, f32[512,384]{1,0:T(8,128)}) fusion(f32[512,384]{1,0:T(8,128)} %fusion.7, f32[512,384]{1,0:T(8,128)} %fusion.5, bf16[512,1024]{1,0:T(8,128)(2,1)} %bitcast.15, bf16[1,384,1024]{2,1,0:T(8,128)(2,1)S(1)} %copy-done), kind=kOutput, calls=%fused_computation.36 | convolution fusion | flops 404422656 | bytes 4980736 | tf_op jit(solution)/shard_map/dot_general | solution.py:8
  49.7 1.7 convolution_bitcast_fusion.1
  51.5 0.2 reduce-scatter.5.cloned.1.call-start
  51.8 3.2 %convolution_bitcast_fusion = f32[1,384,1024]{2,1,0:T(8,128)} fusion(bf16[512,384]{1,0:T(8,128)(2,1)} %get-tuple-element.10, bf16[512,1024]{1,0:T(8,128)(2,1)} %bitcast.15), kind=kOutput, calls=%fused_computation.10 | convolution fusion | flops 402653184 | bytes 3014656 | tf_op jit(solution)/shard_map/dot_general | solution.py:8
  55.0 2.3 %fusion.17 = f32[512,1024]{1,0:T(8,128)S(1)} fusion(bf16[1,384,1024]{2,1,0:T(8,128)(2,1)S(1)} %copy-done.8, f32[512,384]{1,0:T(8,128)} %fusion.7, f32[512,384]{1,0:T(8,128)} %get-tuple-element.13, f32[512,384]{1,0:T(8,128)S(1)} %copy-done.9), kind=kOutput, calls=%fused_computation.33 | convolution fusion | flops 404619264 | bytes 5242880 | tf_op jit(solution)/shard_map/dot_general | solution.py:8
  57.4 0.7 fusion.2
  58.1 1.6 copy.58
  59.7 0.5 broadcast.257
  60.2 7.8 %reduce.2 = bf16[512,1024]{1,0:T(8,128)(2,1)} reduce(bf16[512,1,1024]{2,1,0:T(2,128)(2,1)S(1)} %bitcast.88, bf16[]{:T(256)} %broadcast.257), dimensions={1}, to_apply=%bitcast.82.reduce_sub_computation | reduce | bytes 2097154
  68.0 3.8 %reshape.312 = bf16[4,2,65536]{2,1,0:T(2,128)(2,1)} reshape(bf16[512,1024]{1,0:T(8,128)(2,1)} %reduce.2) | data formatting | bytes 2097152
  71.8 4.5 %all-to-all-start.2 = ((bf16[4,2,65536]{2,1,0:T(2,128)(2,1)}), bf16[4,2,65536]{2,1,0:T(2,128)(2,1)}, u32[]{:S(2)}, u32[]{:S(2)}) async-start(bf16[4,2,65536]{2,1,0:T(2,128)(2,1)} %reshape.312), calls=%async_computation.2 | async-start | bytes 2097152 | tf_op jit(solution)/shard_map/all_to_all | solution.py:86
  76.3 0.7 fusion.1
  77.0 1.6 copy.59
  78.6 7.8 %reduce.1 = bf16[512,1024]{1,0:T(8,128)(2,1)} reduce(bf16[512,1,1024]{2,1,0:T(2,128)(2,1)S(1)} %bitcast.89, bf16[]{:T(256)} %broadcast.257), dimensions={1}, to_apply=%bitcast.83.reduce_sub_computation | reduce | bytes 2097154
  86.4 3.8 %reshape.310 = bf16[4,2,65536]{2,1,0:T(2,128)(2,1)} reshape(bf16[512,1024]{1,0:T(8,128)(2,1)} %reduce.1) | data formatting | bytes 2097152
  90.2 0.3 all-to-all-done.2
  90.6 3.8 %all-to-all-start = ((bf16[4,2,65536]{2,1,0:T(2,128)(2,1)}), bf16[4,2,65536]{2,1,0:T(2,128)(2,1)S(1)}, u32[]{:S(2)}, u32[]{:S(2)}) async-start(bf16[4,2,65536]{2,1,0:T(2,128)(2,1)} %reshape.310), calls=%async_computation | async-start | bytes 2097152 | tf_op jit(solution)/shard_map/all_to_all | solution.py:83
  94.4 0.1 copy.44
  94.5 0.1 mul.94
  94.6 4.0 %reshape.313 = bf16[512,1,1024]{2,1,0:T(2,128)(2,1)} reshape(bf16[4,2,65536]{2,1,0:T(2,128)(2,1)} %all-to-all-done.2) | data formatting | bytes 2097152
  98.6 2.0 %copy.56 = bf16[1,512,1024]{2,1,0:T(8,128)(2,1)S(1)} copy(bf16[1,512,1024]{2,0,1:T(2,128)(2,1)} %bitcast.86) | data formatting | bytes 2097152
  100.6 1.2 gather_fusion.4
  101.7 0.2 gather.28
  101.9 6.5 %all-to-all-done = bf16[4,2,65536]{2,1,0:T(2,128)(2,1)S(1)} async-done(((bf16[4,2,65536]{2,1,0:T(2,128)(2,1)}), bf16[4,2,65536]{2,1,0:T(2,128)(2,1)S(1)}, u32[]{:S(2)}, u32[]{:S(2)}) %all-to-all-start) | async-done | bytes 1048608 | tf_op jit(solution)/shard_map/all_to_all | solution.py:83
  108.5 2.3 %reshape.311 = bf16[512,1,1024]{2,1,0:T(2,128)(2,1)} reshape(bf16[4,2,65536]{2,1,0:T(2,128)(2,1)S(1)} %all-to-all-done) | data formatting | bytes 2097152
  110.8 2.0 %copy.57 = bf16[1,512,1024]{2,1,0:T(8,128)(2,1)S(1)} copy(bf16[1,512,1024]{2,0,1:T(2,128)(2,1)} %bitcast.87) | data formatting | bytes 2097152
  112.7 1.2 gather_fusion.1
  113.9 0.7 reshape.254
  114.6 2.1 %reduce_sum.45 = bf16[128,1024]{1,0:T(8,128)(2,1)} reduce(bf16[128,2,1024]{2,1,0:T(2,128)(2,1)S(1)} %gather.28, bf16[]{:T(256)} %constant.76.clone.1), dimensions={1}, to_apply=%region_5.6 | reduce | flops 131072 | bytes 786434 | tf_op jit(solution)/shard_map/reduce_sum | solution.py:95
  116.7 2.1 %multiply_reduce_fusion = bf16[128,1024]{1,0:T(8,128)(2,1)} fusion(f32[128,2,1024]{2,1,0:T(2,128)S(1)} %reshape.254, f32[128,2]{1,0:T(8,128)S(1)} %copy.45), kind=kLoop, calls=%fused_computation.23 | loop fusion | flops 393216 | bytes 1311744 | tf_op jit(solution)/shard_map/reduce_sum | solution.py:91
  118.7 1.6 broadcast_multiply_fusion.1
  120.3 66.0 %reduce-scatter.5.cloned.1.call-done = f32[1,48,1024]{2,1,0:T(8,128)} async-done(((f32[1,384,1024]{2,1,0:T(8,128)}), f32[1,48,1024]{2,1,0:T(8,128)}) %reduce-scatter.5.cloned.1.call-update) | async-done | bytes 196624 | tf_op jit(solution)/shard_map/reduce_scatter | solution.py:27
  186.4 1.6 broadcast_multiply_fusion
  (45 shorter events, 0.4 us)
Async XLA Ops:
  7.2 39.1 %copy-start = (bf16[1,384,1024]{2,1,0:T(8,128)(2,1)S(1)}, bf16[1,384,1024]{2,1,0:T(8,128)(2,1)}, u32[]{:S(2)}) copy-start(bf16[1,384,1024]{2,1,0:T(8,128)(2,1)} %param.13) | copy-start | bytes 2359300
  7.2 7.6 %copy-start.1 = (bf16[128,1024]{1,0:T(8,128)(2,1)S(1)}, bf16[128,1024]{1,0:T(8,128)(2,1)}, u32[]{:S(2)}) copy-start(bf16[128,1024]{1,0:T(8,128)(2,1)} %param.7) | copy-start | bytes 786436
  17.0 5.5 %copy-start.2 = (bf16[128,1024]{1,0:T(8,128)(2,1)S(1)}, bf16[128,1024]{1,0:T(8,128)(2,1)}, u32[]{:S(2)}) copy-start(bf16[128,1024]{1,0:T(8,128)(2,1)} %param.8) | copy-start | bytes 786436
  17.4 1.0 copy-start.3
  19.2 10.8 %collective-permute-start = (bf16[1,128,1024]{2,1,0:T(8,128)(2,1)S(1)}, bf16[1,128,1024]{2,1,0:T(8,128)(2,1)S(1)}, u32[]{:S(2)}, u32[]{:S(2)}) collective-permute-start(bf16[1,128,1024]{2,1,0:T(8,128)(2,1)S(1)} %get-tuple-element.8), channel_id=1, source_target_pairs={{0,3},{1,0},{2,1},{3,2},{4,7},{5,4},{6,5},{7,6},{8,11},{9,8},{10,9... | collective-permute-start | bytes 786440 | tf_op jit(solution)/shard_map/ppermute | solution.py:79
  21.6 13.3 %collective-permute-start.1 = (bf16[1,128,1024]{2,1,0:T(8,128)(2,1)}, bf16[1,128,1024]{2,1,0:T(8,128)(2,1)S(1)}, u32[]{:S(2)}, u32[]{:S(2)}) collective-permute-start(bf16[1,128,1024]{2,1,0:T(8,128)(2,1)} %get-tuple-element.7), channel_id=1, source_target_pairs={{0,2},{1,3},{2,0},{3,1},{4,6},{5,7},{6,4},{7,5},{8,10},{9,11},{10,... | collective-permute-start | bytes 786440 | tf_op jit(solution)/shard_map/ppermute | solution.py:79
  22.2 12.9 %collective-permute-start.2 = (bf16[1,128,1024]{2,1,0:T(8,128)(2,1)}, bf16[1,128,1024]{2,1,0:T(8,128)(2,1)}, u32[]{:S(2)}, u32[]{:S(2)}) collective-permute-start(bf16[1,128,1024]{2,1,0:T(8,128)(2,1)} %get-tuple-element.6), channel_id=1, source_target_pairs={{0,1},{1,2},{2,3},{3,0},{4,5},{5,6},{6,7},{7,4},{8,9},{9,10},{10,1... | collective-permute-start | bytes 786440 | tf_op jit(solution)/shard_map/ppermute | solution.py:79
  25.7 20.5 %all-to-all-start.1 = ((bf16[4,128,1024]{2,1,0:T(8,128)(2,1)}), bf16[4,128,1024]{2,1,0:T(8,128)(2,1)}, u32[]{:S(2)}, u32[]{:S(2)}) async-start(bf16[4,128,1024]{2,1,0:T(8,128)(2,1)} %fusion), calls=%async_computation.1 | async-start | bytes 2097152 | tf_op jit(solution)/shard_map/all_to_all | solution.py:84
  30.0 88.8 %reduce-scatter.3.cloned.1.call-start = ((), (), s32[]{:S(2)}) async-start(), calls=%async_computation.5 | async-start | bytes 1769472 | tf_op jit(solution)/shard_map/reduce_scatter | solution.py:39
  30.0 9.1 %copy-start.4 = (bf16[1,384,1024]{2,1,0:T(8,128)(2,1)S(1)}, bf16[1,384,1024]{2,1,0:T(8,128)(2,1)}, u32[]{:S(2)}) copy-start(bf16[1,384,1024]{2,1,0:T(8,128)(2,1)} %param.12) | copy-start | bytes 2359300
  37.1 3.7 %copy-start.7 = (bf16[1,384,1024]{2,1,0:T(8,128)(2,1)S(1)}, bf16[1,384,1024]{2,1,0:T(8,128)(2,1)}, u32[]{:S(2)}) copy-start(bf16[1,384,1024]{2,1,0:T(8,128)(2,1)} %param.11) | copy-start | bytes 2359300
  51.5 134.9 %reduce-scatter.5.cloned.1.call-start = ((), (), s32[]{:S(2)}) async-start(), calls=%async_computation.6 | async-start | bytes 1769472 | tf_op jit(solution)/shard_map/reduce_scatter | solution.py:27
  51.7 3.3 %copy-start.8 = (bf16[1,384,1024]{2,1,0:T(8,128)(2,1)S(1)}, bf16[1,384,1024]{2,1,0:T(8,128)(2,1)}, u32[]{:S(2)}) copy-start(bf16[1,384,1024]{2,1,0:T(8,128)(2,1)} %param.11) | copy-start | bytes 2359300
  51.7 3.3 %copy-start.9 = (f32[512,384]{1,0:T(8,128)S(1)}, f32[512,384]{1,0:T(8,128)}, u32[]{:S(2)}) copy-start(f32[512,384]{1,0:T(8,128)} %fusion.5) | copy-start | bytes 2359300
  55.0 2.3 %copy-start.5 = (bf16[1,384,1024]{2,1,0:T(8,128)(2,1)S(1)}, bf16[1,384,1024]{2,1,0:T(8,128)(2,1)}, u32[]{:S(2)}) copy-start(bf16[1,384,1024]{2,1,0:T(8,128)(2,1)} %param.12) | copy-start | bytes 2359300
  68.0 8.2 %copy-start.6 = (bf16[512,384]{1,0:T(8,128)(2,1)S(1)}, bf16[512,384]{1,0:T(8,128)(2,1)}, u32[]{:S(2)}) copy-start(bf16[512,384]{1,0:T(8,128)(2,1)} %get-tuple-element.10) | copy-start | bytes 1179652
  71.8 18.8 %all-to-all-start.2 = ((bf16[4,2,65536]{2,1,0:T(2,128)(2,1)}), bf16[4,2,65536]{2,1,0:T(2,128)(2,1)}, u32[]{:S(2)}, u32[]{:S(2)}) async-start(bf16[4,2,65536]{2,1,0:T(2,128)(2,1)} %reshape.312), calls=%async_computation.2 | async-start | bytes 2097152 | tf_op jit(solution)/shard_map/all_to_all | solution.py:86
  86.4 7.9 %copy-start.10 = (s32[128,2]{0,1:T(2,128)S(1)}, s32[128,2]{0,1:T(2,128)}, u32[]{:S(2)}) copy-start(s32[128,2]{0,1:T(2,128)} %param.9) | copy-start | bytes 3076
  90.6 17.9 %all-to-all-start = ((bf16[4,2,65536]{2,1,0:T(2,128)(2,1)}), bf16[4,2,65536]{2,1,0:T(2,128)(2,1)S(1)}, u32[]{:S(2)}, u32[]{:S(2)}) async-start(bf16[4,2,65536]{2,1,0:T(2,128)(2,1)} %reshape.310), calls=%async_computation | async-start | bytes 2097152 | tf_op jit(solution)/shard_map/all_to_all | solution.py:83
Sparse Core Ops, SparseCore 0:
  51.6 66.6 reduce-scatter.2
  121.8 64.5 reduce-scatter.4
